TPU v7x, 32 devices: a whole 2x2x4 slice. The times are simulated.
32 devices in a mesh: layer: 4 (over y, x), row: 2 (over core), col: 4 (over z).
Axes of the slice: x: 2, y: 2, z: 4, core: 2. Of those that a mesh axis runs over, the one named last changes fastest.
Arguments:
- even_left: bfloat16 [2, 4, 32, 32, 256, 128], P(None, 'layer', 'row', 'col'), may hold values from -0.09375 to 0.09375
- even_right: bfloat16 [2, 4, 32, 32, 256, 128], P(None, 'layer', 'row', 'col'), may hold values from -0.25 to 0.25
- odd_left: bfloat16 [2, 4, 32, 32, 256, 128], P(None, 'layer', 'col', 'row'), may hold values from -0.09375 to 0.09375
- odd_right: bfloat16 [2, 4, 32, 32, 256, 128], P(None, 'layer', 'col', 'row'), may hold values from -0.25 to 0.25
- even_ranks: int32 [2, 4, 32, 32], P(None, 'layer', 'row', 'col'), may hold values from 16 to 64, as said below
- odd_ranks: int32 [2, 4, 32, 32], P(None, 'layer', 'col', 'row'), may hold values from 16 to 64, as said below
- even_sources: float32 [2, 4, 2, 8192, 128], P(None, 'layer', None, ('row', 'col')), may hold values from -6 to 6
- odd_sources: float32 [2, 4, 2, 8192, 128], P(None, 'layer', None, ('col', 'row')), may hold values from -6 to 6
Outputs:
- even_traces: float32 [4, 2, 8192, 128], P('layer', None, ('row', 'col'))
- odd_traces: float32 [4, 2, 8192, 128], P('layer', None, ('col', 'row'))
Inputs may be any that keep to these rules, and one draw needn't show every extreme that they name: `even_ranks`: every direction and pair has a tile of rank 64 and a tile of rank a quarter of 64. `odd_ranks`: every direction and pair has a tile of rank 64 and a tile of rank a quarter of 64.
All inputs are finite; a program needn't handle non-finite values.
Results may differ from a plain program's by a relative error of at most 0.008.
Values may be sent and summed in bfloat16 or wider, within the bound.
A program may use at most 256 MiB of HBM per device.

v0:
```python
import jax
import jax.numpy as jnp
from jax import lax
from jax.sharding import PartitionSpec as P


def shifted(shard, axis, by):
    size = lax.axis_size(axis)
    pairs = [(i, i + by) for i in range(size) if 0 <= i + by < size]
    return lax.ppermute(shard, axis, pairs)


def tile_product(gathered, left_factor, right_factor, tile_ranks):
    batch_count = gathered.shape[0]
    tile_rows, tile_cols, tile_size, twice_rank = right_factor.shape
    half_rank = twice_rank // 2
    width = gathered.shape[2]
    half_cols = width // 2
    traces = gathered.reshape(batch_count, tile_cols, tile_size, width)
    products = jnp.einsum(
        "acnr,kcnb->kacrb", right_factor, traces, preferred_element_type=jnp.float32
    )
    real_part = (
        products[:, :, :, :half_rank, :half_cols] - products[:, :, :, half_rank:, half_cols:]
    )
    imag_part = (
        products[:, :, :, :half_rank, half_cols:] + products[:, :, :, half_rank:, :half_cols]
    )
    rank_mask = (lax.iota(jnp.int32, half_rank)[None, None, :] < tile_ranks[:, :, None]).astype(
        jnp.float32
    )
    rank_mask = rank_mask[None, :, :, :, None]
    real_part = real_part * rank_mask
    imag_part = imag_part * rank_mask
    stacked = jnp.concatenate(
        [
            jnp.concatenate([real_part, imag_part], axis=4),
            jnp.concatenate([-imag_part, real_part], axis=4),
        ],
        axis=3,
    ).astype(jnp.bfloat16)
    result = jnp.einsum(
        "acmr,kacrb->kamb", left_factor, stacked, preferred_element_type=jnp.float32
    )
    return result.reshape(batch_count, tile_rows * tile_size, width)


def on_device(
    even_left, even_right, odd_left, odd_right, even_ranks, odd_ranks, even_sources, odd_sources
):
    segments = lax.axis_size("layer")
    segment_index = lax.axis_index("layer")
    batches = even_sources.shape[2]

    def even_product(gathered, direction):
        return tile_product(
            gathered, even_left[direction, 0], even_right[direction, 0], even_ranks[direction, 0]
        )

    def odd_product(gathered, direction):
        return tile_product(
            gathered, odd_left[direction, 0], odd_right[direction, 0], odd_ranks[direction, 0]
        )

    def even_terms(current, direction):
        gathered = lax.all_gather(current.astype(jnp.bfloat16), "row", axis=1, tiled=True)
        return even_product(gathered, direction)

    def odd_terms(current, direction):
        gathered = lax.all_gather(current.astype(jnp.bfloat16), "col", axis=1, tiled=True)
        return odd_product(gathered, direction)

    def even_reduce(terms):
        return lax.psum_scatter(terms, "col", scatter_dimension=1, tiled=True)

    def odd_reduce(terms):
        return lax.psum_scatter(terms, "row", scatter_dimension=1, tiled=True)

    sources_all = (even_sources[0, 0], odd_sources[0, 0], even_sources[1, 0], odd_sources[1, 0])
    slots = lax.iota(jnp.int32, batches)
    records = [jnp.zeros_like(source) for source in sources_all]
    down_in = jnp.zeros_like(sources_all[1][:1])
    up_in = jnp.zeros_like(sources_all[2][:1])
    total_steps = batches + segments - 1
    for step_index in range(total_steps):
        down_slot = step_index - segment_index
        up_slot = step_index - (segments - 1 - segment_index)
        down_pick = jnp.clip(down_slot, 0, batches - 1)
        up_pick = jnp.clip(up_slot, 0, batches - 1)
        down_even_src = lax.dynamic_slice_in_dim(sources_all[0], down_pick, 1, 0)
        down_odd_src = lax.dynamic_slice_in_dim(sources_all[1], down_pick, 1, 0)
        up_even_src = lax.dynamic_slice_in_dim(sources_all[2], up_pick, 1, 0)
        up_odd_src = lax.dynamic_slice_in_dim(sources_all[3], up_pick, 1, 0)
        down_even = even_reduce(even_terms(down_in, 0)) + down_even_src
        up_odd = odd_reduce(odd_terms(up_in, 1)) + up_odd_src
        advance_down_odd = odd_reduce(odd_terms(down_even, 0)) + down_odd_src
        advance_up_even = even_reduce(even_terms(up_odd, 1)) + up_even_src
        outcome = (down_even, advance_down_odd, advance_up_even, up_odd)
        down_mask = (slots == down_slot)[:, None, None]
        up_mask = (slots == up_slot)[:, None, None]
        records = [
            jnp.where(down_mask, outcome[0], records[0]),
            jnp.where(down_mask, outcome[1], records[1]),
            jnp.where(up_mask, outcome[2], records[2]),
            jnp.where(up_mask, outcome[3], records[3]),
        ]
        if step_index + 1 < total_steps:
            down_odd = outcome[1]
            up_even = outcome[2]
            down_next = shifted(down_odd.astype(jnp.bfloat16), "layer", 1).astype(down_odd.dtype)
            up_next = shifted(up_even.astype(jnp.bfloat16), "layer", -1).astype(up_even.dtype)
            down_in = down_next
            up_in = up_next
    results = tuple(records)
    even_traces = (results[0] + results[2])[None]
    odd_traces = (results[1] + results[3])[None]
    return (even_traces, odd_traces)


def solution(mesh):
    in_specs = (
        P(None, "layer", "row", "col", None, None),
        P(None, "layer", "row", "col", None, None),
        P(None, "layer", "col", "row", None, None),
        P(None, "layer", "col", "row", None, None),
        P(None, "layer", "row", "col"),
        P(None, "layer", "col", "row"),
        P(None, "layer", None, ("row", "col"), None),
        P(None, "layer", None, ("col", "row"), None),
    )
    out_specs = (P("layer", None, ("row", "col"), None), P("layer", None, ("col", "row"), None))
    return jax.shard_map(
        on_device, mesh=mesh, in_specs=in_specs, out_specs=out_specs, check_vma=False
    )
```

profile of v0, /device:TPU:8, one launch (start us, length us, event | category | flops | bytes accessed | tf_op | source)
XLA Modules:
  0.0 1082.3 jit_solution(17235669187562248947)
XLA Ops:
  7.2 12.0 %slice_bitcast_fusion.2 = (bf16[8,16,256,128]{3,2,1,0:T(8,128)(2,1)}, bf16[8,16,256,128]{3,2,1,0:T(8,128)(2,1)}) fusion(bf16[2,1,8,16,256,128]{5,4,3,2,1,0:T(8,128)(2,1)} %param.10), kind=kLoop, calls=%fused_computation.42 | loop fusion | bytes 33554432 | tf_op jit(solution)/shard_map/squeeze | solution.py:62
  19.4 11.9 %fusion.448 = (bf16[1,1,8,16,256,128]{5,4,3,2,1,0:T(8,128)(2,1)}, bf16[1,1,8,16,256,128]{5,4,3,2,1,0:T(8,128)(2,1)}) fusion(bf16[2,1,8,16,256,128]{5,4,3,2,1,0:T(8,128)(2,1)} %param.11), kind=kLoop, calls=%fused_computation.472 | loop fusion | bytes 33554432 | tf_op jit(solution)/shard_map/slice | solution.py:62
  31.2 12.3 %copy.128 = bf16[1,1,8,16,256,128]{4,5,2,3,1,0:T(8,128)(2,1)} copy(bf16[1,1,8,16,256,128]{5,4,3,2,1,0:T(8,128)(2,1)} %get-tuple-element.3) | data formatting | bytes 16777216
  63.2 11.7 %fusion.449 = (bf16[1,1,16,8,256,128]{5,4,3,2,1,0:T(8,128)(2,1)}, bf16[1,1,16,8,256,128]{5,4,3,2,1,0:T(8,128)(2,1)}) fusion(bf16[2,1,16,8,256,128]{5,4,3,2,1,0:T(8,128)(2,1)} %param.9), kind=kLoop, calls=%fused_computation.473 | loop fusion | bytes 33554432 | tf_op jit(solution)/shard_map/slice | solution.py:57
  75.0 11.4 %copy.126 = bf16[1,1,16,8,256,128]{4,5,2,3,1,0:T(8,128)(2,1)} copy(bf16[1,1,16,8,256,128]{5,4,3,2,1,0:T(8,128)(2,1)} %get-tuple-element.6) | data formatting | bytes 16777216
  115.1 11.6 %copy.129 = bf16[1,1,16,8,256,128]{4,5,2,3,1,0:T(8,128)(2,1)} copy(bf16[1,1,16,8,256,128]{5,4,3,2,1,0:T(8,128)(2,1)} %get-tuple-element.7) | data formatting | bytes 16777216
  133.3 25.9 %reduce-scatter.21.cloned.1.call-done = f32[1,1024,128]{2,1,0:T(8,128)} async-done(((f32[1,4096,128]{2,1,0:T(8,128)}), f32[1,1024,128]{2,1,0:T(8,128)}) %reduce-scatter.21.cloned.1.call-update) | async-done | bytes 524304 | tf_op jit(solution)/shard_map/reduce_scatter | solution.py:74
  183.0 12.3 %copy.127 = bf16[1,1,8,16,256,128]{4,5,2,3,1,0:T(8,128)(2,1)} copy(bf16[1,1,8,16,256,128]{5,4,3,2,1,0:T(8,128)(2,1)} %get-tuple-element.2) | data formatting | bytes 16777216
  220.5 13.2 %reduce-scatter.41.cloned.1.call-done = f32[1,1024,128]{2,1,0:T(8,128)} async-done(((f32[1,4096,128]{2,1,0:T(8,128)}), f32[1,1024,128]{2,1,0:T(8,128)}) %reduce-scatter.41.cloned.1.call-update) | async-done | bytes 524304 | tf_op jit(solution)/shard_map/reduce_scatter | solution.py:74
  252.2 22.7 %all-gather.18.cloned.1.call-done = bf16[1,4096,128]{2,1,0:T(8,128)(2,1)} async-done(((bf16[1,1024,128]{2,1,0:T(8,128)(2,1)}), bf16[1,4096,128]{2,1,0:T(8,128)(2,1)}) %all-gather.18.cloned.1.call-update) | async-done | bytes 1048592 | tf_op jit(solution)/shard_map/all_gather | solution.py:70
  327.9 37.7 %reduce-scatter.25.cloned.1.call-done = f32[1,1024,128]{2,1,0:T(8,128)} async-done(((f32[1,4096,128]{2,1,0:T(8,128)}), f32[1,1024,128]{2,1,0:T(8,128)}) %reduce-scatter.25.cloned.1.call-update) | async-done | bytes 524304 | tf_op jit(solution)/shard_map/reduce_scatter | solution.py:74
  420.4 19.7 %reduce-scatter.45.cloned.1.call-done = f32[1,1024,128]{2,1,0:T(8,128)} async-done(((f32[1,4096,128]{2,1,0:T(8,128)}), f32[1,1024,128]{2,1,0:T(8,128)}) %reduce-scatter.45.cloned.1.call-update) | async-done | bytes 524304 | tf_op jit(solution)/shard_map/reduce_scatter | solution.py:74
  458.6 22.9 %all-gather.20.cloned.1.call-done = bf16[1,4096,128]{2,1,0:T(8,128)(2,1)} async-done(((bf16[1,1024,128]{2,1,0:T(8,128)(2,1)}), bf16[1,4096,128]{2,1,0:T(8,128)(2,1)}) %all-gather.20.cloned.1.call-update) | async-done | bytes 1048592 | tf_op jit(solution)/shard_map/all_gather | solution.py:70
  534.5 37.7 %reduce-scatter.29.cloned.1.call-done = f32[1,1024,128]{2,1,0:T(8,128)} async-done(((f32[1,4096,128]{2,1,0:T(8,128)}), f32[1,1024,128]{2,1,0:T(8,128)}) %reduce-scatter.29.cloned.1.call-update) | async-done | bytes 524304 | tf_op jit(solution)/shard_map/reduce_scatter | solution.py:74
  615.8 8.6 fusion.320
  627.0 19.8 %reduce-scatter.49.cloned.1.call-done = f32[1,1024,128]{2,1,0:T(8,128)} async-done(((f32[1,4096,128]{2,1,0:T(8,128)}), f32[1,1024,128]{2,1,0:T(8,128)}) %reduce-scatter.49.cloned.1.call-update) | async-done | bytes 524304 | tf_op jit(solution)/shard_map/reduce_scatter | solution.py:74
  665.2 22.7 %all-gather.22.cloned.1.call-done = bf16[1,4096,128]{2,1,0:T(8,128)(2,1)} async-done(((bf16[1,1024,128]{2,1,0:T(8,128)(2,1)}), bf16[1,4096,128]{2,1,0:T(8,128)(2,1)}) %all-gather.22.cloned.1.call-update) | async-done | bytes 1048592 | tf_op jit(solution)/shard_map/all_gather | solution.py:70
  741.0 37.7 %reduce-scatter.33.cloned.1.call-done = f32[1,1024,128]{2,1,0:T(8,128)} async-done(((f32[1,4096,128]{2,1,0:T(8,128)}), f32[1,1024,128]{2,1,0:T(8,128)}) %reduce-scatter.33.cloned.1.call-update) | async-done | bytes 524304 | tf_op jit(solution)/shard_map/reduce_scatter | solution.py:74
  822.2 8.6 fusion.325
  833.5 19.9 %reduce-scatter.53.cloned.1.call-done = f32[1,1024,128]{2,1,0:T(8,128)} async-done(((f32[1,4096,128]{2,1,0:T(8,128)}), f32[1,1024,128]{2,1,0:T(8,128)}) %reduce-scatter.53.cloned.1.call-update) | async-done | bytes 524304 | tf_op jit(solution)/shard_map/reduce_scatter | solution.py:74
  871.7 23.0 %all-gather.24.cloned.1.call-done = bf16[1,4096,128]{2,1,0:T(8,128)(2,1)} async-done(((bf16[1,1024,128]{2,1,0:T(8,128)(2,1)}), bf16[1,4096,128]{2,1,0:T(8,128)(2,1)}) %all-gather.24.cloned.1.call-update) | async-done | bytes 1048592 | tf_op jit(solution)/shard_map/all_gather | solution.py:70
  947.6 37.7 %reduce-scatter.37.cloned.1.call-done = f32[1,1024,128]{2,1,0:T(8,128)} async-done(((f32[1,4096,128]{2,1,0:T(8,128)}), f32[1,1024,128]{2,1,0:T(8,128)}) %reduce-scatter.37.cloned.1.call-update) | async-done | bytes 524304 | tf_op jit(solution)/shard_map/reduce_scatter | solution.py:74
  1028.8 8.6 fusion.330
  1040.2 19.8 %reduce-scatter.57.cloned.1.call-done = f32[1,1024,128]{2,1,0:T(8,128)} async-done(((f32[1,4096,128]{2,1,0:T(8,128)}), f32[1,1024,128]{2,1,0:T(8,128)}) %reduce-scatter.57.cloned.1.call-update) | async-done | bytes 524304 | tf_op jit(solution)/shard_map/reduce_scatter | solution.py:74
  (263 shorter events, 597.4 us)
Async XLA Ops:
  7.2 121.7 %reduce-scatter.39.cloned.1.call-start = ((), (), s32[]{:S(2)}) async-start(), calls=%async_computation.33 | async-start | bytes 1572864 | tf_op jit(solution)/shard_map/reduce_scatter | solution.py:77
  62.7 96.5 %reduce-scatter.21.cloned.1.call-start = ((), (), s32[]{:S(2)}) async-start(), calls=%async_computation.20 | async-start | bytes 2621440 | tf_op jit(solution)/shard_map/reduce_scatter | solution.py:74
  115.1 80.4 %all-gather.10.cloned.1.call-start = ((), (), s32[]{:S(2)}) async-start(), calls=%async_computation.21 | async-start | bytes 1310720 | tf_op jit(solution)/shard_map/all_gather | solution.py:70
  161.2 72.5 %reduce-scatter.41.cloned.1.call-start = ((), (), s32[]{:S(2)}) async-start(), calls=%async_computation.34 | async-start | bytes 2621440 | tf_op jit(solution)/shard_map/reduce_scatter | solution.py:74
  244.7 78.9 %reduce-scatter.43.cloned.1.call-start = ((), (), s32[]{:S(2)}) async-start(), calls=%async_computation.36 | async-start | bytes 1572864 | tf_op jit(solution)/shard_map/reduce_scatter | solution.py:77
  299.5 66.2 %reduce-scatter.25.cloned.1.call-start = ((), (), s32[]{:S(2)}) async-start(), calls=%async_computation.23 | async-start | bytes 2621440 | tf_op jit(solution)/shard_map/reduce_scatter | solution.py:74
  323.3 72.5 %all-gather.12.cloned.1.call-start = ((), (), s32[]{:S(2)}) async-start(), calls=%async_computation.24 | async-start | bytes 1310720 | tf_op jit(solution)/shard_map/all_gather | solution.py:70
  367.7 72.5 %reduce-scatter.45.cloned.1.call-start = ((), (), s32[]{:S(2)}) async-start(), calls=%async_computation.37 | async-start | bytes 2621440 | tf_op jit(solution)/shard_map/reduce_scatter | solution.py:74
  389.3 61.9 %reduce-scatter.27.cloned.1.call-start = ((), (), s32[]{:S(2)}) async-start(), calls=%async_computation.25 | async-start | bytes 1572864 | tf_op jit(solution)/shard_map/reduce_scatter | solution.py:77
  451.1 79.1 %reduce-scatter.47.cloned.1.call-start = ((), (), s32[]{:S(2)}) async-start(), calls=%async_computation.39 | async-start | bytes 1572864 | tf_op jit(solution)/shard_map/reduce_scatter | solution.py:77
  506.1 66.2 %reduce-scatter.29.cloned.1.call-start = ((), (), s32[]{:S(2)}) async-start(), calls=%async_computation.26 | async-start | bytes 2621440 | tf_op jit(solution)/shard_map/reduce_scatter | solution.py:74
  529.9 72.5 %all-gather.14.cloned.1.call-start = ((), (), s32[]{:S(2)}) async-start(), calls=%async_computation.27 | async-start | bytes 1310720 | tf_op jit(solution)/shard_map/all_gather | solution.py:70
  574.3 72.5 %reduce-scatter.49.cloned.1.call-start = ((), (), s32[]{:S(2)}) async-start(), calls=%async_computation.40 | async-start | bytes 2621440 | tf_op jit(solution)/shard_map/reduce_scatter | solution.py:74
  595.9 61.9 %reduce-scatter.31.cloned.1.call-start = ((), (), s32[]{:S(2)}) async-start(), calls=%async_computation.28 | async-start | bytes 1572864 | tf_op jit(solution)/shard_map/reduce_scatter | solution.py:77
  657.7 78.9 %reduce-scatter.51.cloned.1.call-start = ((), (), s32[]{:S(2)}) async-start(), calls=%async_computation.42 | async-start | bytes 1572864 | tf_op jit(solution)/shard_map/reduce_scatter | solution.py:77
  712.5 66.2 %reduce-scatter.33.cloned.1.call-start = ((), (), s32[]{:S(2)}) async-start(), calls=%async_computation.29 | async-start | bytes 2621440 | tf_op jit(solution)/shard_map/reduce_scatter | solution.py:74
  736.3 72.5 %all-gather.16.cloned.1.call-start = ((), (), s32[]{:S(2)}) async-start(), calls=%async_computation.30 | async-start | bytes 1310720 | tf_op jit(solution)/shard_map/all_gather | solution.py:70
  780.7 72.7 %reduce-scatter.53.cloned.1.call-start = ((), (), s32[]{:S(2)}) async-start(), calls=%async_computation.43 | async-start | bytes 2621440 | tf_op jit(solution)/shard_map/reduce_scatter | solution.py:74
  802.3 62.1 %reduce-scatter.35.cloned.1.call-start = ((), (), s32[]{:S(2)}) async-start(), calls=%async_computation.31 | async-start | bytes 1572864 | tf_op jit(solution)/shard_map/reduce_scatter | solution.py:77
  864.2 78.9 %reduce-scatter.55.cloned.1.call-start = ((), (), s32[]{:S(2)}) async-start(), calls=%async_computation.45 | async-start | bytes 1572864 | tf_op jit(solution)/shard_map/reduce_scatter | solution.py:77
  919.2 66.1 %reduce-scatter.37.cloned.1.call-start = ((), (), s32[]{:S(2)}) async-start(), calls=%async_computation.32 | async-start | bytes 2621440 | tf_op jit(solution)/shard_map/reduce_scatter | solution.py:74
  942.9 72.5 %all-gather.26.cloned.1.call-start = ((), (), s32[]{:S(2)}) async-start(), calls=%async_computation.47 | async-start | bytes 1310720 | tf_op jit(solution)/shard_map/all_gather | solution.py:70
  987.3 72.6 %reduce-scatter.57.cloned.1.call-start = ((), (), s32[]{:S(2)}) async-start(), calls=%async_computation.46 | async-start | bytes 2621440 | tf_op jit(solution)/shard_map/reduce_scatter | solution.py:74
  1008.8 62.1 %reduce-scatter.59.cloned.1.call-start = ((), (), s32[]{:S(2)}) async-start(), calls=%async_computation.48 | async-start | bytes 1572864 | tf_op jit(solution)/shard_map/reduce_scatter | solution.py:77
  (27 other events, 694.4 us)
Sparse Core Ops, SparseCore 0:
  62.8 9.8 reduce-scatter.38
  115.2 43.9 reduce-scatter.20
  161.3 27.9 all-gather.9
  191.5 42.1 reduce-scatter.40
  235.8 8.7 reduce-scatter.22
  246.0 28.8 all-gather.17
  323.4 42.1 reduce-scatter.24
  367.8 27.9 all-gather.11
  397.9 42.1 reduce-scatter.44
  442.4 8.7 reduce-scatter.26
  452.6 28.8 all-gather.19
  530.0 42.1 reduce-scatter.28
  574.4 27.9 all-gather.13
  604.5 42.1 reduce-scatter.48
  648.9 8.7 reduce-scatter.30
  659.1 28.8 all-gather.21
  736.4 42.1 reduce-scatter.32
  780.8 27.9 all-gather.15
  811.1 42.1 reduce-scatter.52
  855.6 8.7 reduce-scatter.34
  865.8 28.8 all-gather.23
  943.1 42.1 reduce-scatter.36
  987.4 27.9 all-gather.25
  1017.7 42.1 reduce-scatter.56
  (5 shorter events, 40.9 us)
where the time goes:
time: 1090 us; the launch traced here: 1080 us
  waiting for transfers between devices  424 us (39%)
  matrix products  268 us (25%)
  other arithmetic  181 us (17%)
  local copies, waits for them, and re-layouts  144 us (13%)
  starting transfers between devices  29.1 us (3%)
  blocking collectives  21.1 us (2%)
  between operations  15.3 us (1%)
    reduce_scatter x10, waiting for transfers between devices, even_reduce(): return lax.psum_scatter(terms, 'col', scatter_dimension=1, tiled=True)  269 us
    dot_general x20, matrix products, tile_product(): jnp.einsum('acmr,kacrb->kamb', left_factor, stacked, preferred_element_ty...  149 us
    dot_general x20, matrix products, tile_product(): jnp.einsum('acnr,kcnb->kacrb', right_factor, traces, preferred_element_ty...  119 us
    all_gather x9, waiting for transfers between devices, odd_terms(): lax.all_gather(current.astype(jnp.bfloat16), 'col', axis=1, tiled=True)  117 us
    another operation x20, other arithmetic  72.7 us
    concatenate x20, other arithmetic, tile_product(): jnp.concatenate([jnp.concatenate([real_part, imag_part], axis=4), jnp.con...  62 us
    transpose x20, local copies, waits for them, and re-layouts, tile_product(): jnp.einsum('acmr,kacrb->kamb', left_factor, stacked, preferred_element_ty...  52.4 us
    unnamed x32, local copies, waits for them, and re-layouts  48.5 us
  transfers between devices with their start and end apart: 37, of which 25 were waited for; matrix products, arithmetic and copies ran while one was open for 48% of the time, Pallas kernels for 0%

commit v1 on v0

v1 whole, which is shorter than its diff:
```python
import functools

import jax
import jax.numpy as jnp
from jax import lax
from jax.experimental import pallas as pl
from jax.experimental.pallas import tpu as pltpu
from jax.sharding import PartitionSpec as P

MESH = pl.DeviceIdType.MESH


def product_kernel(rows_per, flag_ref, rank_ref, x_ref, v_ref, u_ref, y_ref, xt_ref):
    step = pl.program_id(0)
    cols, tile, twice = v_ref.shape[3], v_ref.shape[4], v_ref.shape[5]
    width = x_ref.shape[1]
    half, batch = twice // 2, width // 2

    @pl.when(flag_ref[0] > 0)
    def _():
        @pl.when(step == 0)
        def _():
            for c in range(cols):
                block = x_ref[c * tile : (c + 1) * tile, :].astype(jnp.float32)
                xt_ref[c] = block.T.astype(jnp.bfloat16)

        lane = lax.broadcasted_iota(jnp.int32, (1, twice), 1)
        sign = jnp.where(lane < half, 1.0, -1.0).astype(jnp.float32)
        within = jnp.where(lane < half, lane, lane - half)
        group = 2 if cols % 2 == 0 else 1
        pair = 2 if rows_per % 2 == 0 else 1
        for a in range(0, rows_per, pair):
            totals = [jnp.zeros((width, tile), jnp.float32) for _ in range(pair)]
            for c in range(0, cols, group):
                stacked = [[None] * group for _ in range(pair)]
                for g in range(group):
                    right = jnp.concatenate([v_ref[0, 0, a + j, c + g] for j in range(pair)], axis=1)
                    coeff = jnp.dot(xt_ref[c + g], right, preferred_element_type=jnp.float32)
                    for j in range(pair):
                        rank = rank_ref[(step * rows_per + a + j) * cols + c + g]
                        mask = (within < rank).astype(jnp.float32)
                        part = coeff[:, j * twice : (j + 1) * twice]
                        top = (part[:batch] * sign - pltpu.roll(part[batch:], half, 1)) * mask
                        low = pltpu.roll(top, half, 1) * (-sign)
                        stacked[j][g] = jnp.concatenate([top, low], axis=0).astype(jnp.bfloat16)
                for j in range(pair):
                    left = jnp.concatenate([u_ref[0, 0, a + j, c + g] for g in range(group)], axis=1)
                    totals[j] += lax.dot_general(
                        jnp.concatenate(stacked[j], axis=1),
                        left,
                        (((1,), (1,)), ((), ())),
                        preferred_element_type=jnp.float32,
                    )
            for j in range(pair):
                y_ref[(a + j) * tile : (a + j + 1) * tile, :] = totals[j].T.astype(y_ref.dtype)


def product(flag, ranks, x, right, left, direction):
    _, _, rows, cols, tile, twice = right.shape
    width = x.shape[1]
    rows_per = 2 if rows % 2 == 0 else 1

    def factor_map(i, flag_ref, rank_ref):
        return (direction, 0, jnp.where(flag_ref[0] > 0, i, 0), 0, 0, 0)

    factor = pl.BlockSpec((1, 1, rows_per, cols, tile, twice), factor_map)
    return pl.pallas_call(
        functools.partial(product_kernel, rows_per),
        out_shape=jax.ShapeDtypeStruct((rows * tile, width), jnp.bfloat16),
        grid_spec=pltpu.PrefetchScalarGridSpec(
            num_scalar_prefetch=2,
            grid=(rows // rows_per,),
            in_specs=[pl.BlockSpec((cols * tile, width), lambda i, f, r: (0, 0)), factor, factor],
            out_specs=pl.BlockSpec((rows_per * tile, width), lambda i, f, r: (i, 0)),
            scratch_shapes=[pltpu.VMEM((cols, width, tile), jnp.bfloat16)],
        ),
        compiler_params=pltpu.CompilerParams(vmem_limit_bytes=40 * 1024 * 1024),
        cost_estimate=pl.CostEstimate(
            flops=4 * rows * cols * tile * twice * width,
            bytes_accessed=4 * rows * cols * tile * twice,
            transcendentals=0,
        ),
        name="tile_product",
    )(flag, ranks, x, right, left)


def peer(axis, offset):
    size = lax.axis_size(axis)
    return lax.rem(lax.axis_index(axis) + offset, size)


def exchange_kernel(spec, *refs):
    step, batches, segments, sides, use_y, edge, last = spec
    refs = list(refs)
    layer = lax.axis_index("layer")
    take = lambda count: [refs.pop(0) for _ in range(count)]
    y_refs = take(2) if use_y else [None, None]
    src_refs = take(2)
    total_refs = take(2)
    x_refs = [None, None] if last else take(2)
    src_bufs, landing = take(2), take(2)
    hand = take(2) if edge and not last else [None, None]
    src_sem, rs_send, rs_recv = take(1)[0], take(2), take(2)
    ag_send, ag_recv = ([None, None], [None, None]) if last else (take(2), take(2))
    shift_send, shift_recv = take(2) if edge and not last else (None, None)

    plan = []
    for side in range(2):
        direction, rs_axis, ag_axis = sides[side]
        distance = layer if direction > 0 else segments - 1 - layer
        slot = step - distance
        active = (slot >= 0) & (slot < batches)
        have_y = active if edge else active & (distance > 0)
        sends = active & (distance < segments - 1)
        receives = (slot + 1 >= 0) & (slot + 1 < batches) & (distance > 0)
        plan.append((direction, rs_axis, ag_axis, slot, active, have_y, sends, receives))

    barrier = pltpu.get_barrier_semaphore()
    expect = 0
    for axis in ("row", "col"):
        for k in range(1, lax.axis_size(axis)):
            pl.semaphore_signal(
                barrier, inc=1, device_id={axis: peer(axis, k)}, device_id_type=MESH
            )
            expect += 1
    expect = jnp.int32(expect)
    if edge and not last:
        for direction, _, _, _, _, _, sends, receives in plan:

            @pl.when(receives)
            def _(direction=direction):
                pl.semaphore_signal(
                    barrier, inc=1, device_id={"layer": layer - direction}, device_id_type=MESH
                )

            expect = expect + jnp.where(sends, 1, 0)

    def source_copy(side):
        slot = plan[side][3]
        direction = 0 if plan[side][0] > 0 else 1
        return pltpu.make_async_copy(
            src_refs[side].at[direction, 0, slot], src_bufs[side], src_sem.at[side]
        )

    for side in range(2):

        @pl.when(plan[side][4])
        def _(side=side):
            source_copy(side).start()

    pl.semaphore_wait(barrier, expect)
    shard = src_bufs[0].shape[0]

    def rs_copy(side, k):
        target = peer(plan[side][1], k)
        return pltpu.make_async_remote_copy(
            src_ref=y_refs[side].at[pl.ds(pl.multiple_of(target * shard, shard), shard)],
            dst_ref=landing[side].at[k - 1],
            send_sem=rs_send[side].at[k - 1],
            recv_sem=rs_recv[side].at[k - 1],
            device_id={plan[side][1]: target},
            device_id_type=MESH,
        )

    def ag_own(side):
        own = lax.axis_index(plan[side][2])
        return x_refs[side].at[pl.ds(pl.multiple_of(own * shard, shard), shard)]

    def ag_copy(side, k):
        return pltpu.make_async_remote_copy(
            src_ref=ag_own(side),
            dst_ref=ag_own(side),
            send_sem=ag_send[side].at[k - 1],
            recv_sem=ag_recv[side].at[k - 1],
            device_id={plan[side][2]: peer(plan[side][2], k)},
            device_id_type=MESH,
        )

    def shift_copy(side):
        return pltpu.make_async_remote_copy(
            src_ref=hand[side],
            dst_ref=ag_own(side),
            send_sem=shift_send.at[side],
            recv_sem=shift_recv.at[side],
            device_id={"layer": layer + plan[side][0]},
            device_id_type=MESH,
        )

    def peers(axis):
        return range(1, lax.axis_size(axis))

    order = sorted(range(2), key=lambda side: 0 if sides[side][1] == "row" else 1)
    for side in order:
        if use_y:

            @pl.when(plan[side][5])
            def _(side=side):
                for k in peers(plan[side][1]):
                    rs_copy(side, k).start()

    for side in order:
        direction, rs_axis, ag_axis, slot, active, have_y, sends, receives = plan[side]

        @pl.when(active)
        def _(side=side):
            source_copy(side).wait()

        if use_y:

            @pl.when(have_y)
            def _(side=side, rs_axis=rs_axis):
                for k in peers(rs_axis):
                    rs_copy(side, k).wait_recv()
                own = pl.multiple_of(lax.axis_index(rs_axis) * shard, shard)
                value = src_bufs[side][...] + y_refs[side][pl.ds(own, shard), :].astype(jnp.float32)
                for k in peers(rs_axis):
                    value = value + landing[side][k - 1].astype(jnp.float32)
                total_refs[side][...] = value

            plain = active & jnp.logical_not(have_y)
        else:
            plain = active
        if not edge:

            @pl.when(plain)
            def _(side=side):
                total_refs[side][...] = src_bufs[side][...]

            @pl.when(active)
            def _(side=side, ag_axis=ag_axis):
                own = pl.multiple_of(lax.axis_index(ag_axis) * shard, shard)
                x_refs[side][pl.ds(own, shard), :] = total_refs[side][...].astype(jnp.bfloat16)
                for k in peers(ag_axis):
                    ag_copy(side, k).start()

        elif not last:

            @pl.when(sends)
            def _(side=side):
                hand[side][...] = total_refs[side][...].astype(jnp.bfloat16)
                shift_copy(side).start()

    if edge and not last:
        for side in order:

            @pl.when(plan[side][7])
            def _(side=side):
                shift_copy(side).wait_recv()
                for k in peers(plan[side][2]):
                    ag_copy(side, k).start()

    for side in order:
        if use_y:

            @pl.when(plan[side][5])
            def _(side=side):
                for k in peers(plan[side][1]):
                    rs_copy(side, k).wait_send()

        if last:
            continue
        if edge:

            @pl.when(plan[side][6])
            def _(side=side):
                shift_copy(side).wait_send()

        @pl.when(plan[side][7] if edge else plan[side][4])
        def _(side=side):
            for k in peers(plan[side][2]):
                ag_copy(side, k).wait()


def exchange(step, edge, last, y_pair, src_pair, collective_id):
    batches = src_pair[0].shape[2]
    shard, width = src_pair[0].shape[3:]
    segments = lax.axis_size("layer")
    if edge:
        sides = ((1, "row", "row"), (-1, "col", "col"))
    else:
        sides = ((1, "col", "col"), (-1, "row", "row"))
    use_y = y_pair is not None
    spec = (step, batches, segments, sides, use_y, edge, last)
    operands = (list(y_pair) if use_y else []) + list(src_pair)
    vmem = pl.BlockSpec(memory_space=pltpu.VMEM)
    anywhere = pl.BlockSpec(memory_space=pl.ANY)
    in_specs = ([vmem] * 2 if use_y else []) + [anywhere] * 2
    outs = [jax.ShapeDtypeStruct((shard, width), jnp.float32)] * 2
    if not last:
        outs += [
            jax.ShapeDtypeStruct((lax.axis_size(side[2]) * shard, width), jnp.bfloat16)
            for side in sides
        ]
    count = [max(lax.axis_size(side[1]) - 1, 1) for side in sides]
    scratch = [pltpu.VMEM((shard, width), jnp.float32)] * 2
    scratch += [pltpu.VMEM((n, shard, width), jnp.bfloat16) for n in count]
    if edge and not last:
        scratch += [pltpu.VMEM((shard, width), jnp.bfloat16)] * 2
    scratch += [pltpu.SemaphoreType.DMA((2,))]
    scratch += [pltpu.SemaphoreType.DMA((n,)) for n in count] * 2
    if not last:
        scratch += [pltpu.SemaphoreType.DMA((n,)) for n in count] * 2
    if edge and not last:
        scratch += [pltpu.SemaphoreType.DMA((2,))] * 2
    return pl.pallas_call(
        functools.partial(exchange_kernel, spec),
        out_shape=outs,
        in_specs=in_specs,
        out_specs=[vmem] * len(outs),
        scratch_shapes=scratch,
        compiler_params=pltpu.CompilerParams(
            collective_id=collective_id,
            has_side_effects=True,
            vmem_limit_bytes=40 * 1024 * 1024,
        ),
        name="exchange_edge" if edge else "exchange_mid",
    )(*operands)


def on_device(
    even_left, even_right, odd_left, odd_right, even_ranks, odd_ranks, even_sources, odd_sources
):
    segments = lax.axis_size("layer")
    layer = lax.axis_index("layer")
    batches = even_sources.shape[2]
    even_flat = [even_ranks[e, 0].reshape(-1) for e in range(2)]
    odd_flat = [odd_ranks[e, 0].reshape(-1) for e in range(2)]

    def flag(slot, skip):
        active = (slot >= 0) & (slot < batches) & jnp.logical_not(skip)
        return active.astype(jnp.int32).reshape(1)

    never = jnp.bool_(False)
    history = []
    x_down = x_up = None
    total_steps = batches + segments - 1
    for step in range(total_steps):
        down_slot = step - layer
        up_slot = step - (segments - 1 - layer)
        last = step + 1 == total_steps
        if step == 0:
            y_pair = None
        else:
            y_pair = (
                product(
                    flag(down_slot, layer == 0), even_flat[0], x_down, even_right, even_left, 0
                ),
                product(
                    flag(up_slot, layer == segments - 1), odd_flat[1], x_up, odd_right, odd_left, 1
                ),
            )
        down_even, up_odd, x_down, x_up = exchange(
            step, False, False, y_pair, (even_sources, odd_sources), 2 * step
        )
        y_pair = (
            product(flag(down_slot, never), odd_flat[0], x_down, odd_right, odd_left, 0),
            product(flag(up_slot, never), even_flat[1], x_up, even_right, even_left, 1),
        )
        result = exchange(step, True, last, y_pair, (odd_sources, even_sources), 2 * step + 1)
        down_odd, up_even = result[:2]
        if not last:
            x_down, x_up = result[2:]
        history.append((down_even, down_odd, up_even, up_odd))

    def chosen(which, batch, distance):
        picked = history[batch][which]
        for away in range(1, segments):
            picked = jnp.where(distance == away, history[batch + away][which], picked)
        return picked

    up_distance = segments - 1 - layer
    even_traces = jnp.stack(
        [chosen(0, m, layer) + chosen(2, m, up_distance) for m in range(batches)]
    )[None]
    odd_traces = jnp.stack(
        [chosen(1, m, layer) + chosen(3, m, up_distance) for m in range(batches)]
    )[None]
    return (even_traces, odd_traces)


def solution(mesh):
    in_specs = (
        P(None, "layer", "row", "col", None, None),
        P(None, "layer", "row", "col", None, None),
        P(None, "layer", "col", "row", None, None),
        P(None, "layer", "col", "row", None, None),
        P(None, "layer", "row", "col"),
        P(None, "layer", "col", "row"),
        P(None, "layer", None, ("row", "col"), None),
        P(None, "layer", None, ("col", "row"), None),
    )
    out_specs = (P("layer", None, ("row", "col"), None), P("layer", None, ("col", "row"), None))
    return jax.shard_map(
        on_device, mesh=mesh, in_specs=in_specs, out_specs=out_specs, check_vma=False
    )
```

time: 1090 us -> 564 us (0.52)
  Pallas kernels: 0 us -> 501 us
  waiting for transfers between devices: 424 us -> 0 us
  matrix products: 268 us -> 0 us
  other arithmetic: 181 us -> 6.56 us
  local copies, waits for them, and re-layouts: 144 us -> 54.1 us
  starting transfers between devices: 29.1 us -> 0 us
  blocking collectives: 21.1 us -> 0 us
  between operations: 15.3 us -> 1.01 us
    pallas_call x0 -> x28, Pallas kernels: none -> 501 us  [the longest x10 391 us: exchange(): pl.pallas_call(functools.partial(exchange_kernel, spec), out_shape=outs,...]
    reduce_scatter x20 -> x0, waiting for transfers between devices: 276 us -> none  [the longest x10 269 us: even_reduce(): return lax.psum_scatter(terms, 'col', scatter_dimension=1, tiled=True)]
    dot_general x40 -> x0, matrix products: 268 us -> none  [the longest x20 149 us: tile_product(): jnp.einsum('acmr,kacrb->kamb', left_factor, stacked, preferred_element_ty...]
    all_gather x9 -> x0, waiting for transfers between devices: 117 us -> none  [odd_terms(): lax.all_gather(current.astype(jnp.bfloat16), 'col', axis=1, tiled=True)]
    another operation x20 -> x2, other arithmetic: 72.7 us -> 5.11 us  [the longest x1 2.56 us: on_device(): jnp.stack([chosen(0, m, layer) + chosen(2, m, up_distance) for m in range...]
    concatenate x20 -> x0, other arithmetic: 62 us -> none  [tile_product(): jnp.concatenate([jnp.concatenate([real_part, imag_part], axis=4), jnp.con...]
    transpose x20 -> x0, local copies, waits for them, and re-layouts: 52.4 us -> none  [tile_product(): jnp.einsum('acmr,kacrb->kamb', left_factor, stacked, preferred_element_ty...]
    ppermute x8 -> x0, waiting for transfers between devices: 30.6 us -> none  [shifted(): return lax.ppermute(shard, axis, pairs)]
  transfers between devices with their start and end apart: 37 -> 0, of which waited for: 25 -> 0; matrix products, arithmetic and copies ran while one was open for 48% -> 0% of each run, Pallas kernels for 0% -> 0%
where the time goes in v1:
time: 564 us; the launch traced here: 562 us
  Pallas kernels  501 us (89%)
  local copies, waits for them, and re-layouts  54.1 us (10%)
  other arithmetic  6.56 us (1%)
    pallas_call x10, Pallas kernels, exchange(): pl.pallas_call(functools.partial(exchange_kernel, spec), out_shape=outs,...  391 us
    pallas_call x18, Pallas kernels, product(): pl.pallas_call(functools.partial(product_kernel, rows_per), out_shape=jax...  110 us
    unnamed x134, local copies, waits for them, and re-layouts  52.9 us

profile of v1, /device:TPU:8, one launch (start us, length us, event | category | flops | bytes accessed | tf_op | source)
XLA Modules:
  0.0 562.3 jit_solution(6843081455625380687)
XLA Ops:
  4.7 26.3 %exchange_mid.5 = (f32[1024,128]{1,0:T(8,128)S(1)}, f32[1024,128]{1,0:T(8,128)S(1)}, bf16[4096,128]{1,0:T(8,128)(2,1)S(1)}, bf16[2048,128]{1,0:T(8,128)(2,1)S(1)}) custom-call(f32[2,1,2,1024,128]{4,3,2,1,0:T(8,128)S(1)} %copy-done, f32[2,1,2,1024,128]{4,3,2,1,0:T(8,128)S(1)} %copy-done.2), custom_call_target="tpu_custom_call" | custom-call | tf_op jit(solution)/shard_map/exchange_mid/pallas_call | solution.py:305
  37.0 13.7 %tile_product.18.refs_0_ = bf16[2048,128]{1,0:T(8,128)(2,1)S(1)} custom-call(s32[1]{0:T(128)} %bitcast.5.flag_ref, s32[128]{0:T(128)S(1)} %reshape_squeeze.13.rank_ref, bf16[4096,128]{1,0:T(8,128)(2,1)S(1)} %copy-done.21, bf16[2,1,8,16,256,128]{5,4,3,2,1,0:T(8,128)(2,1)} %v_ref.34, bf16[2,1,8,16,256,128]{5,4,3,2,1,0:T(8,128)(2,1)} %u_ref.34), custom_call_target="tpu_custom_call" | custom-call | flops 2147483648 | bytes 16777216 | tf_op jit(solution)/shard_map/tile_product/pallas_call | solution.py:67
  50.7 8.5 %exchange_edge.5 = (f32[1024,128]{1,0:T(8,128)S(1)}, f32[1024,128]{1,0:T(8,128)S(1)}, bf16[2048,128]{1,0:T(8,128)(2,1)S(1)}, bf16[4096,128]{1,0:T(8,128)(2,1)S(1)}) custom-call(bf16[2048,128]{1,0:T(8,128)(2,1)S(1)} %tile_product.18.refs_0_, bf16[4096,128]{1,0:T(8,128)(2,1)S(1)} %tile_product.19.refs_1_, f32[2,1,2,1024,128]{4,3,2,1,0:T(8,128)S(1)} %copy-done.3, ...), custom_call_target="tpu_custom_call" | custom-call | tf_op jit(solution)/shard_map/exchange_edge/pallas_call | solution.py:305
  64.0 2.8 tile_product.21.refs_1_
  66.9 2.2 tile_product.20.refs_0_
  69.1 27.2 %exchange_mid.6 = (f32[1024,128]{1,0:T(8,128)S(1)}, f32[1024,128]{1,0:T(8,128)S(1)}, bf16[4096,128]{1,0:T(8,128)(2,1)S(1)}, bf16[2048,128]{1,0:T(8,128)(2,1)S(1)}) custom-call(bf16[4096,128]{1,0:T(8,128)(2,1)S(1)} %tile_product.20.refs_0_, bf16[2048,128]{1,0:T(8,128)(2,1)S(1)} %tile_product.21.refs_1_, f32[2,1,2,1024,128]{4,3,2,1,0:T(8,128)S(1)} %copy-done.1, ...), custom_call_target="tpu_custom_call" | custom-call | tf_op jit(solution)/shard_map/exchange_mid/pallas_call | solution.py:305
  104.1 13.5 %tile_product.22.refs_0_ = bf16[2048,128]{1,0:T(8,128)(2,1)S(1)} custom-call(s32[1]{0:T(128)} %bitcast.3.flag_ref, s32[128]{0:T(128)S(1)} %reshape_squeeze.13.rank_ref, bf16[4096,128]{1,0:T(8,128)(2,1)S(1)} %copy-done.25, bf16[2,1,8,16,256,128]{5,4,3,2,1,0:T(8,128)(2,1)} %v_ref.34, bf16[2,1,8,16,256,128]{5,4,3,2,1,0:T(8,128)(2,1)} %u_ref.34), custom_call_target="tpu_custom_call" | custom-call | flops 2147483648 | bytes 16777216 | tf_op jit(solution)/shard_map/tile_product/pallas_call | solution.py:67
  117.6 43.5 %exchange_edge.6 = (f32[1024,128]{1,0:T(8,128)S(1)}, f32[1024,128]{1,0:T(8,128)S(1)}, bf16[2048,128]{1,0:T(8,128)(2,1)S(1)}, bf16[4096,128]{1,0:T(8,128)(2,1)S(1)}) custom-call(bf16[2048,128]{1,0:T(8,128)(2,1)S(1)} %tile_product.22.refs_0_, bf16[4096,128]{1,0:T(8,128)(2,1)S(1)} %tile_product.23.refs_1_, f32[2,1,2,1024,128]{4,3,2,1,0:T(8,128)S(1)} %copy-done.5, ...), custom_call_target="tpu_custom_call" | custom-call | tf_op jit(solution)/shard_map/exchange_edge/pallas_call | solution.py:305
  168.9 2.9 tile_product.25.refs_1_
  171.8 2.6 exchange_mid.7
  182.1 2.9 tile_product.26.refs_0_
  185.0 189.0 %exchange_edge.7 = (f32[1024,128]{1,0:T(8,128)S(1)}, f32[1024,128]{1,0:T(8,128)S(1)}, bf16[2048,128]{1,0:T(8,128)(2,1)S(1)}, bf16[4096,128]{1,0:T(8,128)(2,1)S(1)}) custom-call(bf16[2048,128]{1,0:T(8,128)(2,1)S(1)} %tile_product.26.refs_0_, bf16[4096,128]{1,0:T(8,128)(2,1)S(1)} %tile_product.27.refs_1_, f32[2,1,2,1024,128]{4,3,2,1,0:T(8,128)S(1)} %copy-done.7, ...), custom_call_target="tpu_custom_call" | custom-call | tf_op jit(solution)/shard_map/exchange_edge/pallas_call | solution.py:305
  381.7 13.5 %tile_product.29.refs_1_ = bf16[2048,128]{1,0:T(8,128)(2,1)S(1)} custom-call(s32[1]{0:T(128)} %bitcast.11.flag_ref, s32[128]{0:T(128)S(1)} %reshape_squeeze.15.rank_ref, bf16[4096,128]{1,0:T(8,128)(2,1)S(1)} %copy-done.17, bf16[2,1,8,16,256,128]{5,4,3,2,1,0:T(8,128)(2,1)} %v_ref.34, bf16[2,1,8,16,256,128]{5,4,3,2,1,0:T(8,128)(2,1)} %u_ref.34), custom_call_target="tpu_custom_call" | custom-call | flops 2147483648 | bytes 16777216 | tf_op jit(solution)/shard_map/tile_product/pallas_call | solution.py:67
  395.2 6.3 %exchange_mid.8 = (f32[1024,128]{1,0:T(8,128)S(1)}, f32[1024,128]{1,0:T(8,128)S(1)}, bf16[4096,128]{1,0:T(8,128)(2,1)S(1)}, bf16[2048,128]{1,0:T(8,128)(2,1)S(1)}) custom-call(bf16[4096,128]{1,0:T(8,128)(2,1)S(1)} %tile_product.28.refs_0_, bf16[2048,128]{1,0:T(8,128)(2,1)S(1)} %tile_product.29.refs_1_, f32[2,1,2,1024,128]{4,3,2,1,0:T(8,128)S(1)} %copy-done.1, ...), custom_call_target="tpu_custom_call" | custom-call | tf_op jit(solution)/shard_map/exchange_mid/pallas_call | solution.py:305
  405.9 13.5 %tile_product.31.refs_1_ = bf16[4096,128]{1,0:T(8,128)(2,1)S(1)} custom-call(s32[1]{0:T(128)} %bitcast.13.flag_ref, s32[128]{0:T(128)S(1)} %reshape_squeeze.14.rank_ref, bf16[2048,128]{1,0:T(8,128)(2,1)S(1)} %copy-done.45, bf16[2,1,16,8,256,128]{5,4,3,2,1,0:T(8,128)(2,1)} %v_ref.35, bf16[2,1,16,8,256,128]{5,4,3,2,1,0:T(8,128)(2,1)} %u_ref.35), custom_call_target="tpu_custom_call" | custom-call | flops 2147483648 | bytes 16777216 | tf_op jit(solution)/shard_map/tile_product/pallas_call | solution.py:67
  420.7 2.9 tile_product.30.refs_0_
  423.5 54.5 %exchange_edge.8 = (f32[1024,128]{1,0:T(8,128)S(1)}, f32[1024,128]{1,0:T(8,128)S(1)}, bf16[2048,128]{1,0:T(8,128)(2,1)S(1)}, bf16[4096,128]{1,0:T(8,128)(2,1)S(1)}) custom-call(bf16[2048,128]{1,0:T(8,128)(2,1)S(1)} %tile_product.30.refs_0_, bf16[4096,128]{1,0:T(8,128)(2,1)S(1)} %tile_product.31.refs_1_, f32[2,1,2,1024,128]{4,3,2,1,0:T(8,128)S(1)} %copy-done.9, ...), custom_call_target="tpu_custom_call" | custom-call | tf_op jit(solution)/shard_map/exchange_edge/pallas_call | solution.py:305
  485.9 13.5 %tile_product.33.refs_1_ = bf16[2048,128]{1,0:T(8,128)(2,1)S(1)} custom-call(s32[1]{0:T(128)} %bitcast.16.flag_ref, s32[128]{0:T(128)S(1)} %reshape_squeeze.15.rank_ref, bf16[4096,128]{1,0:T(8,128)(2,1)S(1)} %copy-done.13, bf16[2,1,8,16,256,128]{5,4,3,2,1,0:T(8,128)(2,1)} %v_ref.34, bf16[2,1,8,16,256,128]{5,4,3,2,1,0:T(8,128)(2,1)} %u_ref.34), custom_call_target="tpu_custom_call" | custom-call | flops 2147483648 | bytes 16777216 | tf_op jit(solution)/shard_map/tile_product/pallas_call | solution.py:67
  499.4 6.3 %exchange_mid.9 = (f32[1024,128]{1,0:T(8,128)S(1)}, f32[1024,128]{1,0:T(8,128)S(1)}, bf16[4096,128]{1,0:T(8,128)(2,1)S(1)}, bf16[2048,128]{1,0:T(8,128)(2,1)S(1)}) custom-call(bf16[4096,128]{1,0:T(8,128)(2,1)S(1)} %tile_product.32.refs_0_, bf16[2048,128]{1,0:T(8,128)(2,1)S(1)} %tile_product.33.refs_1_, f32[2,1,2,1024,128]{4,3,2,1,0:T(8,128)S(1)} %copy-done.1, ...), custom_call_target="tpu_custom_call" | custom-call | tf_op jit(solution)/shard_map/exchange_mid/pallas_call | solution.py:305
  510.2 13.5 %tile_product.35.refs_1_ = bf16[4096,128]{1,0:T(8,128)(2,1)S(1)} custom-call(s32[1]{0:T(128)} %bitcast.18.flag_ref, s32[128]{0:T(128)S(1)} %reshape_squeeze.14.rank_ref, bf16[2048,128]{1,0:T(8,128)(2,1)S(1)} %copy-done.39, bf16[2,1,16,8,256,128]{5,4,3,2,1,0:T(8,128)(2,1)} %v_ref.35, bf16[2,1,16,8,256,128]{5,4,3,2,1,0:T(8,128)(2,1)} %u_ref.35), custom_call_target="tpu_custom_call" | custom-call | flops 2147483648 | bytes 16777216 | tf_op jit(solution)/shard_map/tile_product/pallas_call | solution.py:67
  524.9 2.9 tile_product.34.refs_0_
  527.7 26.4 %exchange_edge.9 = (f32[1024,128]{1,0:T(8,128)S(1)}, f32[1024,128]{1,0:T(8,128)S(1)}) custom-call(bf16[2048,128]{1,0:T(8,128)(2,1)S(1)} %tile_product.34.refs_0_, bf16[4096,128]{1,0:T(8,128)(2,1)S(1)} %tile_product.35.refs_1_, f32[2,1,2,1024,128]{4,3,2,1,0:T(8,128)S(1)} %copy-done.11, f32[2,1,2,1024,128]{4,3,2,1,0:T(8,128)S(1)} %copy-done.1), custom_call_target="tpu_custom_call" | custom-call | tf_op jit(solution)/shard_map/exchange_edge/pallas_call | solution.py:305
  555.7 2.5 add_bitcast_fusion.1
  558.3 2.6 add_bitcast_fusion.3
  (149 shorter events, 68.1 us)
Async XLA Ops:
  1.5 1.6 copy-start
  3.1 1.6 copy-start.2
  33.6 2.1 copy-start.66
  35.8 1.2 copy-start.21
  37.0 13.7 %copy-start.1 = (f32[2,1,2,1024,128]{4,3,2,1,0:T(8,128)S(1)}, f32[2,1,2,1024,128]{4,3,2,1,0:T(8,128)}, u32[]{:S(2)}) copy-start(f32[2,1,2,1024,128]{4,3,2,1,0:T(8,128)} %refs_3_.17) | copy-start | bytes 6291460
  37.0 13.7 %copy-start.3 = (f32[2,1,2,1024,128]{4,3,2,1,0:T(8,128)S(1)}, f32[2,1,2,1024,128]{4,3,2,1,0:T(8,128)}, u32[]{:S(2)}) copy-start(f32[2,1,2,1024,128]{4,3,2,1,0:T(8,128)} %refs_2_.17) | copy-start | bytes 6291460
  62.8 1.2 copy-start.19
  64.0 2.9 copy-start.31
  66.9 2.2 copy-start.4
  99.7 1.0 copy-start.41
  102.9 1.2 copy-start.25
  104.1 13.5 %copy-start.5 = (f32[2,1,2,1024,128]{4,3,2,1,0:T(8,128)S(1)}, f32[2,1,2,1024,128]{4,3,2,1,0:T(8,128)}, u32[]{:S(2)}) copy-start(f32[2,1,2,1024,128]{4,3,2,1,0:T(8,128)} %refs_2_.17) | copy-start | bytes 6291460
  167.7 1.2 copy-start.15
  168.9 2.9 copy-start.6
  180.9 1.2 copy-start.27
  182.1 2.9 copy-start.7
  380.5 1.2 copy-start.17
  381.7 13.5 %copy-start.8 = (f32[2,1,2,1024,128]{4,3,2,1,0:T(8,128)S(1)}, f32[2,1,2,1024,128]{4,3,2,1,0:T(8,128)}, u32[]{:S(2)}) copy-start(f32[2,1,2,1024,128]{4,3,2,1,0:T(8,128)} %refs_2_.17) | copy-start | bytes 6291460
  419.4 1.2 copy-start.29
  420.7 2.9 copy-start.9
  484.6 1.2 copy-start.13
  485.9 13.5 %copy-start.10 = (f32[2,1,2,1024,128]{4,3,2,1,0:T(8,128)S(1)}, f32[2,1,2,1024,128]{4,3,2,1,0:T(8,128)}, u32[]{:S(2)}) copy-start(f32[2,1,2,1024,128]{4,3,2,1,0:T(8,128)} %refs_2_.17) | copy-start | bytes 6291460
  523.7 1.2 copy-start.23
  524.9 2.9 copy-start.11
  (43 other events, 37.7 us)

commit v2 on v1

--- a/solution.py
+++ b/solution.py
@@ -70,11 +70,11 @@
         grid_spec=pltpu.PrefetchScalarGridSpec(
             num_scalar_prefetch=2,
             grid=(rows // rows_per,),
-            in_specs=[pl.BlockSpec((cols * tile, width), lambda i, f, r: (0, 0)), factor, factor],
+            in_specs=[pl.BlockSpec(memory_space=pltpu.VMEM), factor, factor],
             out_specs=pl.BlockSpec((rows_per * tile, width), lambda i, f, r: (i, 0)),
             scratch_shapes=[pltpu.VMEM((cols, width, tile), jnp.bfloat16)],
         ),
-        compiler_params=pltpu.CompilerParams(vmem_limit_bytes=40 * 1024 * 1024),
+        compiler_params=pltpu.CompilerParams(vmem_limit_bytes=50 * 1024 * 1024),
         cost_estimate=pl.CostEstimate(
             flops=4 * rows * cols * tile * twice * width,
             bytes_accessed=4 * rows * cols * tile * twice,
@@ -96,9 +96,10 @@
     take = lambda count: [refs.pop(0) for _ in range(count)]
     y_refs = take(2) if use_y else [None, None]
     src_refs = take(2)
-    total_refs = take(2)
+    total_outs = take(2)
     x_refs = [None, None] if last else take(2)
-    src_bufs, landing = take(2), take(2)
+    src_bufs, landing, total_refs = take(2), take(2), take(2)
+    out_sem = take(1)[0]
     hand = take(2) if edge and not last else [None, None]
     src_sem, rs_send, rs_recv = take(1)[0], take(2), take(2)
     ag_send, ag_recv = ([None, None], [None, None]) if last else (take(2), take(2))
@@ -135,6 +136,9 @@
 
             expect = expect + jnp.where(sends, 1, 0)
 
+    def total_copy(side):
+        return pltpu.make_async_copy(total_refs[side], total_outs[side], out_sem.at[side])
+
     def source_copy(side):
         slot = plan[side][3]
         direction = 0 if plan[side][0] > 0 else 1
@@ -220,7 +224,13 @@
             plain = active & jnp.logical_not(have_y)
         else:
             plain = active
-        if not edge:
+        if edge:
+
+            @pl.when(active)
+            def _(side=side):
+                total_copy(side).start()
+
+        else:
 
             @pl.when(plain)
             def _(side=side):
@@ -228,12 +238,13 @@
 
             @pl.when(active)
             def _(side=side, ag_axis=ag_axis):
+                total_copy(side).start()
                 own = pl.multiple_of(lax.axis_index(ag_axis) * shard, shard)
                 x_refs[side][pl.ds(own, shard), :] = total_refs[side][...].astype(jnp.bfloat16)
                 for k in peers(ag_axis):
                     ag_copy(side, k).start()
 
-        elif not last:
+        if edge and not last:
 
             @pl.when(sends)
             def _(side=side):
@@ -250,6 +261,11 @@
                     ag_copy(side, k).start()
 
     for side in order:
+
+        @pl.when(plan[side][4])
+        def _(side=side):
+            total_copy(side).wait()
+
         if use_y:
 
             @pl.when(plan[side][5])
@@ -283,7 +299,7 @@
     spec = (step, batches, segments, sides, use_y, edge, last)
     operands = (list(y_pair) if use_y else []) + list(src_pair)
     vmem = pl.BlockSpec(memory_space=pltpu.VMEM)
-    anywhere = pl.BlockSpec(memory_space=pl.ANY)
+    anywhere = pl.BlockSpec(memory_space=pltpu.HBM)
     in_specs = ([vmem] * 2 if use_y else []) + [anywhere] * 2
     outs = [jax.ShapeDtypeStruct((shard, width), jnp.float32)] * 2
     if not last:
@@ -294,6 +310,8 @@
     count = [max(lax.axis_size(side[1]) - 1, 1) for side in sides]
     scratch = [pltpu.VMEM((shard, width), jnp.float32)] * 2
     scratch += [pltpu.VMEM((n, shard, width), jnp.bfloat16) for n in count]
+    scratch += [pltpu.VMEM((shard, width), jnp.float32)] * 2
+    scratch += [pltpu.SemaphoreType.DMA((2,))]
     if edge and not last:
         scratch += [pltpu.VMEM((shard, width), jnp.bfloat16)] * 2
     scratch += [pltpu.SemaphoreType.DMA((2,))]
@@ -306,12 +324,12 @@
         functools.partial(exchange_kernel, spec),
         out_shape=outs,
         in_specs=in_specs,
-        out_specs=[vmem] * len(outs),
+        out_specs=[anywhere] * 2 + [vmem] * (len(outs) - 2),
         scratch_shapes=scratch,
         compiler_params=pltpu.CompilerParams(
             collective_id=collective_id,
             has_side_effects=True,
-            vmem_limit_bytes=40 * 1024 * 1024,
+            vmem_limit_bytes=50 * 1024 * 1024,
         ),
         name="exchange_edge" if edge else "exchange_mid",
     )(*operands)

time: 564 us -> 540 us (0.957)
  local copies, waits for them, and re-layouts: 54.1 us -> 21.8 us
  Pallas kernels: 501 us -> 510 us
    unnamed x134 -> x54, local copies, waits for them, and re-layouts: 52.9 us -> 20.6 us
    pallas_call x10, Pallas kernels: 391 us -> 400 us  [exchange(): pl.pallas_call(functools.partial(exchange_kernel, spec), out_shape=outs,...]
where the time goes in v2:
time: 540 us; the launch traced here: 538 us
  Pallas kernels  510 us (94%)
  local copies, waits for them, and re-layouts  21.8 us (4%)
  other arithmetic  6.1 us (1%)
    pallas_call x10, Pallas kernels, exchange(): pl.pallas_call(functools.partial(exchange_kernel, spec), out_shape=outs,...  400 us
    pallas_call x18, Pallas kernels, product(): pl.pallas_call(functools.partial(product_kernel, rows_per), out_shape=jax...  109 us
    unnamed x54, local copies, waits for them, and re-layouts  20.6 us

profile of v2, /device:TPU:8, one launch (start us, length us, event | category | flops | bytes accessed | tf_op | source)
XLA Modules:
  0.0 538.4 jit_solution(13233000599848849245)
XLA Ops:
  1.5 26.4 %exchange_mid.5 = (f32[1024,128]{1,0:T(8,128)S(1)}, f32[1024,128]{1,0:T(8,128)S(1)}, bf16[4096,128]{1,0:T(8,128)(2,1)S(1)}, bf16[2048,128]{1,0:T(8,128)(2,1)S(1)}) custom-call(f32[2,1,2,1024,128]{4,3,2,1,0:T(8,128)} %refs_3_.17, f32[2,1,2,1024,128]{4,3,2,1,0:T(8,128)} %refs_2_.17), custom_call_target="tpu_custom_call" | custom-call | tf_op jit(solution)/shard_map/exchange_mid/pallas_call | solution.py:323
  28.0 2.1 tile_product.19.refs_1_
  31.1 13.4 %tile_product.18.refs_0_ = bf16[2048,128]{1,0:T(8,128)(2,1)S(1)} custom-call(s32[1]{0:T(128)} %bitcast.5.flag_ref, s32[128]{0:T(128)S(1)} %reshape_squeeze.13.rank_ref, bf16[4096,128]{1,0:T(8,128)(2,1)S(1)} %get-tuple-element.40.x_ref, bf16[2,1,8,16,256,128]{5,4,3,2,1,0:T(8,128)(2,1)} %v_ref.34, bf16[2,1,8,16,256,128]{5,4,3,2,1,0:T(8,128)(2,1)} %u_ref.34), custom_call_target="tpu_custom_call" | custom-call | flops 2147483648 | bytes 16777216 | tf_op jit(solution)/shard_map/tile_product/pallas_call | solution.py:67
  44.6 9.8 %exchange_edge.5 = (f32[1024,128]{1,0:T(8,128)S(1)}, f32[1024,128]{1,0:T(8,128)S(1)}, bf16[2048,128]{1,0:T(8,128)(2,1)S(1)}, bf16[4096,128]{1,0:T(8,128)(2,1)S(1)}) custom-call(bf16[2048,128]{1,0:T(8,128)(2,1)S(1)} %tile_product.18.refs_0_, bf16[4096,128]{1,0:T(8,128)(2,1)} %copy-done.1, f32[2,1,2,1024,128]{4,3,2,1,0:T(8,128)} %refs_2_.17, ...), custom_call_target="tpu_custom_call" | custom-call | tf_op jit(solution)/shard_map/exchange_edge/pallas_call | solution.py:323
  56.0 2.8 tile_product.21.refs_1_
  62.0 28.5 %exchange_mid.6 = (f32[1024,128]{1,0:T(8,128)S(1)}, f32[1024,128]{1,0:T(8,128)S(1)}, bf16[4096,128]{1,0:T(8,128)(2,1)S(1)}, bf16[2048,128]{1,0:T(8,128)(2,1)S(1)}) custom-call(bf16[4096,128]{1,0:T(8,128)(2,1)} %copy-done.7, bf16[2048,128]{1,0:T(8,128)(2,1)S(1)} %tile_product.21.refs_1_, f32[2,1,2,1024,128]{4,3,2,1,0:T(8,128)} %refs_3_.17, ...), custom_call_target="tpu_custom_call" | custom-call | tf_op jit(solution)/shard_map/exchange_mid/pallas_call | solution.py:323
  95.2 13.4 %tile_product.22.refs_0_ = bf16[2048,128]{1,0:T(8,128)(2,1)S(1)} custom-call(s32[1]{0:T(128)} %bitcast.3.flag_ref, s32[128]{0:T(128)S(1)} %reshape_squeeze.13.rank_ref, bf16[4096,128]{1,0:T(8,128)(2,1)S(1)} %get-tuple-element.44.x_ref, bf16[2,1,8,16,256,128]{5,4,3,2,1,0:T(8,128)(2,1)} %v_ref.34, bf16[2,1,8,16,256,128]{5,4,3,2,1,0:T(8,128)(2,1)} %u_ref.34), custom_call_target="tpu_custom_call" | custom-call | flops 2147483648 | bytes 16777216 | tf_op jit(solution)/shard_map/tile_product/pallas_call | solution.py:67
  108.6 44.7 %exchange_edge.6 = (f32[1024,128]{1,0:T(8,128)S(1)}, f32[1024,128]{1,0:T(8,128)S(1)}, bf16[2048,128]{1,0:T(8,128)(2,1)S(1)}, bf16[4096,128]{1,0:T(8,128)(2,1)S(1)}) custom-call(bf16[2048,128]{1,0:T(8,128)(2,1)S(1)} %tile_product.22.refs_0_, bf16[4096,128]{1,0:T(8,128)(2,1)} %copy-done.4, f32[2,1,2,1024,128]{4,3,2,1,0:T(8,128)} %refs_2_.17, ...), custom_call_target="tpu_custom_call" | custom-call | tf_op jit(solution)/shard_map/exchange_edge/pallas_call | solution.py:323
  158.0 2.8 tile_product.25.refs_1_
  160.7 3.9 exchange_mid.7
  169.3 2.8 tile_product.26.refs_0_
  172.1 189.9 %exchange_edge.7 = (f32[1024,128]{1,0:T(8,128)S(1)}, f32[1024,128]{1,0:T(8,128)S(1)}, bf16[2048,128]{1,0:T(8,128)(2,1)S(1)}, bf16[4096,128]{1,0:T(8,128)(2,1)S(1)}) custom-call(bf16[2048,128]{1,0:T(8,128)(2,1)S(1)} %tile_product.26.refs_0_, bf16[4096,128]{1,0:T(8,128)(2,1)} %copy-done.5, f32[2,1,2,1024,128]{4,3,2,1,0:T(8,128)} %refs_2_.17, ...), custom_call_target="tpu_custom_call" | custom-call | tf_op jit(solution)/shard_map/exchange_edge/pallas_call | solution.py:323
  366.7 13.4 %tile_product.29.refs_1_ = bf16[2048,128]{1,0:T(8,128)(2,1)S(1)} custom-call(s32[1]{0:T(128)} %bitcast.11.flag_ref, s32[128]{0:T(128)S(1)} %reshape_squeeze.15.rank_ref, bf16[4096,128]{1,0:T(8,128)(2,1)S(1)} %get-tuple-element.51.x_ref, bf16[2,1,8,16,256,128]{5,4,3,2,1,0:T(8,128)(2,1)} %v_ref.34, bf16[2,1,8,16,256,128]{5,4,3,2,1,0:T(8,128)(2,1)} %u_ref.34), custom_call_target="tpu_custom_call" | custom-call | flops 2147483648 | bytes 16777216 | tf_op jit(solution)/shard_map/tile_product/pallas_call | solution.py:67
  380.1 7.5 %exchange_mid.8 = (f32[1024,128]{1,0:T(8,128)S(1)}, f32[1024,128]{1,0:T(8,128)S(1)}, bf16[4096,128]{1,0:T(8,128)(2,1)S(1)}, bf16[2048,128]{1,0:T(8,128)(2,1)S(1)}) custom-call(bf16[4096,128]{1,0:T(8,128)(2,1)} %copy-done.3, bf16[2048,128]{1,0:T(8,128)(2,1)S(1)} %tile_product.29.refs_1_, f32[2,1,2,1024,128]{4,3,2,1,0:T(8,128)} %refs_3_.17, ...), custom_call_target="tpu_custom_call" | custom-call | tf_op jit(solution)/shard_map/exchange_mid/pallas_call | solution.py:323
  389.3 13.5 %tile_product.31.refs_1_ = bf16[4096,128]{1,0:T(8,128)(2,1)S(1)} custom-call(s32[1]{0:T(128)} %bitcast.13.flag_ref, s32[128]{0:T(128)S(1)} %reshape_squeeze.14.rank_ref, bf16[2048,128]{1,0:T(8,128)(2,1)S(1)} %get-tuple-element.57.x_ref, bf16[2,1,16,8,256,128]{5,4,3,2,1,0:T(8,128)(2,1)} %v_ref.35, bf16[2,1,16,8,256,128]{5,4,3,2,1,0:T(8,128)(2,1)} %u_ref.35), custom_call_target="tpu_custom_call" | custom-call | flops 2147483648 | bytes 16777216 | tf_op jit(solution)/shard_map/tile_product/pallas_call | solution.py:67
  403.7 2.8 tile_product.30.refs_0_
  406.5 55.8 %exchange_edge.8 = (f32[1024,128]{1,0:T(8,128)S(1)}, f32[1024,128]{1,0:T(8,128)S(1)}, bf16[2048,128]{1,0:T(8,128)(2,1)S(1)}, bf16[4096,128]{1,0:T(8,128)(2,1)S(1)}) custom-call(bf16[2048,128]{1,0:T(8,128)(2,1)S(1)} %tile_product.30.refs_0_, bf16[4096,128]{1,0:T(8,128)(2,1)} %copy-done.6, f32[2,1,2,1024,128]{4,3,2,1,0:T(8,128)} %refs_2_.17, ...), custom_call_target="tpu_custom_call" | custom-call | tf_op jit(solution)/shard_map/exchange_edge/pallas_call | solution.py:323
  467.0 13.4 %tile_product.33.refs_1_ = bf16[2048,128]{1,0:T(8,128)(2,1)S(1)} custom-call(s32[1]{0:T(128)} %bitcast.16.flag_ref, s32[128]{0:T(128)S(1)} %reshape_squeeze.15.rank_ref, bf16[4096,128]{1,0:T(8,128)(2,1)S(1)} %get-tuple-element.63.x_ref, bf16[2,1,8,16,256,128]{5,4,3,2,1,0:T(8,128)(2,1)} %v_ref.34, bf16[2,1,8,16,256,128]{5,4,3,2,1,0:T(8,128)(2,1)} %u_ref.34), custom_call_target="tpu_custom_call" | custom-call | flops 2147483648 | bytes 16777216 | tf_op jit(solution)/shard_map/tile_product/pallas_call | solution.py:67
  480.4 7.5 %exchange_mid.9 = (f32[1024,128]{1,0:T(8,128)S(1)}, f32[1024,128]{1,0:T(8,128)S(1)}, bf16[4096,128]{1,0:T(8,128)(2,1)S(1)}, bf16[2048,128]{1,0:T(8,128)(2,1)S(1)}) custom-call(bf16[4096,128]{1,0:T(8,128)(2,1)} %copy-done, bf16[2048,128]{1,0:T(8,128)(2,1)S(1)} %tile_product.33.refs_1_, f32[2,1,2,1024,128]{4,3,2,1,0:T(8,128)} %refs_3_.17, ...), custom_call_target="tpu_custom_call" | custom-call | tf_op jit(solution)/shard_map/exchange_mid/pallas_call | solution.py:323
  489.6 13.5 %tile_product.35.refs_1_ = bf16[4096,128]{1,0:T(8,128)(2,1)S(1)} custom-call(s32[1]{0:T(128)} %bitcast.18.flag_ref, s32[128]{0:T(128)S(1)} %reshape_squeeze.14.rank_ref, bf16[2048,128]{1,0:T(8,128)(2,1)S(1)} %get-tuple-element.66.x_ref, bf16[2,1,16,8,256,128]{5,4,3,2,1,0:T(8,128)(2,1)} %v_ref.35, bf16[2,1,16,8,256,128]{5,4,3,2,1,0:T(8,128)(2,1)} %u_ref.35), custom_call_target="tpu_custom_call" | custom-call | flops 2147483648 | bytes 16777216 | tf_op jit(solution)/shard_map/tile_product/pallas_call | solution.py:67
  503.1 2.8 tile_product.34.refs_0_
  505.9 26.4 %exchange_edge.9 = (f32[1024,128]{1,0:T(8,128)S(1)}, f32[1024,128]{1,0:T(8,128)S(1)}) custom-call(bf16[2048,128]{1,0:T(8,128)(2,1)S(1)} %tile_product.34.refs_0_, bf16[4096,128]{1,0:T(8,128)(2,1)S(1)} %tile_product.35.refs_1_, f32[2,1,2,1024,128]{4,3,2,1,0:T(8,128)} %refs_2_.17, f32[2,1,2,1024,128]{4,3,2,1,0:T(8,128)} %refs_3_.17), custom_call_target="tpu_custom_call" | custom-call | tf_op jit(solution)/shard_map/exchange_edge/pallas_call | solution.py:323
  532.3 2.4 add_bitcast_fusion.1
  534.7 2.2 add_bitcast_fusion.3
  (69 shorter events, 35.8 us)
Async XLA Ops:
  27.9 2.1 copy-start.8
  28.0 3.1 copy-start.26
  30.1 1.0 copy-start.1
  54.3 0.8 copy-start.10
  55.1 0.8 copy-start.11
  61.1 1.0 copy-start.7
  90.5 0.8 copy-start.12
  94.2 1.0 copy-start.4
  153.3 0.8 copy-start.13
  154.1 0.8 copy-start.15
  157.0 1.0 copy-start.2
  164.7 0.8 copy-start.16
  168.4 1.0 copy-start.5
  362.0 0.8 copy-start.17
  362.8 0.8 copy-start.19
  365.7 1.0 copy-start.3
  387.7 0.8 copy-start.20
  388.5 0.8 copy-start.22
  402.8 1.0 copy-start.6
  462.3 0.8 copy-start.21
  466.0 1.0 copy-start
  487.9 0.8 copy-start.24
  488.7 0.9 copy-start.25
  503.1 29.3 %copy-start.9 = (f32[1024,128]{1,0:T(8,128)S(1)}, f32[1024,128]{1,0:T(8,128)}, u32[]{:S(2)}) copy-start(f32[1024,128]{1,0:T(8,128)} %copy-done.8) | copy-start | bytes 1572868
  (3 other events, 2.4 us)
